TPU v7x, 256 devices: a whole 4x4x8 slice. The times are simulated.
256 devices in a mesh: ctx: 64 (over x, y, z_lo), tp: 4 (over z_hi, core).
Axes of the slice: x: 4, y: 4, z: 8 (z_hi: 2, z_lo: 4; z = z_hi * 4 + z_lo), core: 2. Of those that a mesh axis runs over, the one named last changes fastest.
Arguments:
- span_rows: bfloat16 [2, 2048, 3584], P(None, 'ctx'), may hold values from -6 to 6
- step_rows: bfloat16 [4, 256, 3584], P(None, 'ctx'), may hold values from -6 to 6
- lengths: int32 [2], replicated, may hold values from 4097 to 6144
- sample_prompt: int32 [256], P('ctx'), may hold values from 0 to 1
- norm_gain: float32 [3584], replicated, may hold values from 0.5 to 1.5
- query_weight: bfloat16 [3584, 3584], P('ctx', 'tp'), may hold values from -0.1875 to 0.1875
- key_weight: bfloat16 [3584, 512], P(None, 'tp'), may hold values from -0.1875 to 0.1875
- value_weight: bfloat16 [3584, 512], P(None, 'tp'), may hold values from -0.09375 to 0.09375
- query_bias: float32 [3584], P('tp'), may hold values from -16 to 16
- key_bias: float32 [512], P('tp'), may hold values from -16 to 16
- value_bias: float32 [512], P('tp'), may hold values from -3 to 3
- out_weight: bfloat16 [3584, 3584], P('tp', 'ctx'), may hold values from -0.25 to 0.25
- cache_keys: bfloat16 [2, 4096, 512], P(None, 'ctx', 'tp'), may hold values from -12 to 12
- cache_values: bfloat16 [2, 4096, 512], P(None, 'ctx', 'tp'), may hold values from -6 to 6
Outputs:
- span_out: bfloat16 [2, 2048, 3584], P(None, 'ctx', 'tp')
- dec_out: bfloat16 [4, 256, 3584], P(None, 'ctx', 'tp')
All inputs are finite; a program needn't handle non-finite values.
Results may differ from a plain program's by a relative error of at most 0.012.
The roundings to bfloat16 on the way count: a program that leaves them out, or rounds other values in their place, can miss the bound.
Values may be sent and summed in bfloat16 or wider, within the bound.
A program may use at most 128 MiB of HBM per device.

v0:
```python
import math

import jax
import jax.numpy as jnp
from jax import lax
from jax.sharding import PartitionSpec as P

HEADS = 28
KV_HEADS = 4
HEAD = 128


ROPE_BASE = 1000000.0
NORM_EPS = 1e-06
MASKED = -1e30


def turned_gather(arrays, axis, dims):
    turned = [jnp.moveaxis(a, dim, 0) for a, dim in zip(arrays, dims)]
    widths = [t[0].size for t in turned]
    both = jnp.concatenate([t.reshape(-1, w) for t, w in zip(turned, widths)], axis=1)
    filled = lax.all_gather(both, axis, axis=0, tiled=True)
    parts = jnp.split(filled, [sum(widths[:k]) for k in range(1, len(widths))], axis=1)
    return tuple(
        (
            jnp.moveaxis(b.reshape(-1, *t.shape[1:]), 0, dim)
            for b, t, dim in zip(parts, turned, dims)
        )
    )


def sent_together(arrays, axis, dim, along):
    widths = [a.shape[along] for a in arrays]
    both = jnp.concatenate(arrays, axis=along)
    filled = lax.all_gather(both, axis, axis=dim, tiled=True)
    return tuple(jnp.split(filled, [sum(widths[:k]) for k in range(1, len(widths))], axis=along))


def in_blocks(x, dim, length):
    before, after = (x.shape[:dim], x.shape[dim + 1 :])
    return jnp.moveaxis(x.reshape(*before, length, -1, *after), dim, 0)


def sum_at_owner(x, axis, dim):
    parts = in_blocks(x, dim, lax.axis_size(axis))
    arrived = lax.all_to_all(parts, axis, split_axis=0, concat_axis=0, tiled=True)
    return arrived.astype(jnp.float32).sum(axis=0)


def norm_rows(inputs, norm_gain):
    widened = inputs.astype(jnp.float32)
    inverse = lax.rsqrt(jnp.mean(widened * widened, axis=-1, keepdims=True) + NORM_EPS)
    return (widened * inverse * norm_gain).astype(jnp.bfloat16)


def rotate(vectors, positions):
    width = vectors.shape[-1]
    half = width // 2
    exponent = jnp.arange(half, dtype=jnp.float32) * (2.0 / width)
    frequency = jnp.exp(exponent * -math.log(ROPE_BASE))
    angles = positions.astype(jnp.float32)[..., None, None] * frequency
    cosine = jnp.cos(angles)
    sine = jnp.sin(angles)
    first = vectors[..., :half]
    second = vectors[..., half:]
    return jnp.concatenate(
        [first * cosine - second * sine, second * cosine + first * sine], axis=-1
    )


def project(normed, weight, bias):
    return jnp.dot(normed, weight, preferred_element_type=jnp.float32) + bias


def key_positions(count, prefix_dev, span_dev, prefix_all):
    row_index = jnp.arange(count, dtype=jnp.int32)
    device = row_index // (prefix_dev + span_dev)
    offset = row_index % (prefix_dev + span_dev)
    return jnp.where(
        offset < prefix_dev,
        device * prefix_dev + offset,
        prefix_all + device * span_dev + offset - prefix_dev,
    )


def local(
    span_rows,
    step_rows,
    lengths,
    sample_prompt,
    norm_gain,
    query_weight,
    key_weight,
    value_weight,
    query_bias,
    key_bias,
    value_bias,
    out_weight,
    cache_keys,
    cache_values,
):
    cycle_size = lax.axis_size("ctx")
    cycle_place = lax.axis_index("ctx")
    prompt_count = span_rows.shape[0]
    span_dev = span_rows.shape[1]
    prefix_dev = cache_keys.shape[1]
    kv_local = key_weight.shape[1] // HEAD
    kv_group = HEADS // KV_HEADS
    heads_local = kv_local * kv_group
    prefix_all = prefix_dev * cycle_size
    factor = HEAD ** (-0.5)
    full_query, full_out = turned_gather((query_weight, out_weight), "ctx", (0, 1))
    normed = norm_rows(span_rows, norm_gain)
    span_places = prefix_all + cycle_place * span_dev + jnp.arange(span_dev, dtype=jnp.int32)
    grid_places = jnp.broadcast_to(span_places, (prompt_count, span_dev))
    queries = rotate(
        project(normed, full_query, query_bias).reshape(prompt_count, span_dev, heads_local, HEAD),
        grid_places,
    ).astype(jnp.bfloat16)
    new_keys = rotate(
        project(normed, key_weight, key_bias).reshape(prompt_count, span_dev, kv_local, HEAD),
        grid_places,
    ).astype(jnp.bfloat16)
    new_values = project(normed, value_weight, value_bias).astype(jnp.bfloat16)
    key_block = jnp.concatenate(
        [cache_keys, new_keys.reshape(prompt_count, span_dev, kv_local * HEAD)], axis=1
    )
    value_block = jnp.concatenate([cache_values, new_values], axis=1)
    query_rows = (
        queries.reshape(prompt_count, span_dev, kv_local, kv_group, HEAD)
        .transpose(0, 2, 1, 3, 4)
        .reshape(prompt_count, kv_local, span_dev * kv_group, HEAD)
    )
    query_places = jnp.repeat(span_places, kv_group)
    row_count = span_dev * kv_group
    key_all, value_all = sent_together((key_block, value_block), "ctx", 1, 0)
    highest = jnp.full((prompt_count, kv_local, row_count), MASKED, jnp.float32)
    count = key_all.shape[1]
    places = key_positions(count, prefix_dev, span_dev, prefix_all)
    key_grid = key_all.reshape(prompt_count, count, kv_local, HEAD)
    value_grid = value_all.reshape(prompt_count, count, kv_local, HEAD)
    scores = (
        jnp.einsum("pgqd,pkgd->pgqk", query_rows, key_grid, preferred_element_type=jnp.float32)
        * factor
    )
    visible = (places[None, None, None, :] < lengths[:, None, None, None]) & (
        places[None, None, None, :] <= query_places[None, None, :, None]
    )
    scores = jnp.where(visible, scores, MASKED)
    raised = jnp.maximum(highest, jnp.max(scores, axis=-1))
    weights = jnp.where(visible, jnp.exp(scores - raised[..., None]), 0.0)
    totals = jnp.sum(weights, axis=-1)
    blended = jnp.einsum(
        "pgqk,pkgd->pgqd",
        weights.astype(jnp.bfloat16),
        value_grid,
        preferred_element_type=jnp.float32,
    )
    highest, totals, blended = (raised, totals, blended)
    span_attention = (blended / totals[..., None]).astype(jnp.bfloat16)
    span_attention = (
        span_attention.reshape(prompt_count, kv_local, span_dev, kv_group, HEAD)
        .transpose(0, 2, 1, 3, 4)
        .reshape(prompt_count, span_dev, heads_local * HEAD)
    )
    span_terms = jnp.dot(span_attention, full_out, preferred_element_type=jnp.float32)
    span_out = sum_at_owner(span_terms.astype(jnp.bfloat16), "tp", 2).astype(jnp.bfloat16)
    gathered_rows = key_all.shape[1]
    key_grid = key_all.reshape(prompt_count, gathered_rows, kv_local, HEAD)
    value_grid = value_all.reshape(prompt_count, gathered_rows, kv_local, HEAD)
    all_places = key_positions(gathered_rows, prefix_dev, span_dev, prefix_all)
    picked = sample_prompt[:, None] == jnp.arange(prompt_count, dtype=jnp.int32)[None, :]
    length_of = jnp.sum(jnp.where(picked, lengths[None, :], 0), axis=1)
    prefix_visible = picked[:, :, None] & (all_places[None, None, :] < length_of[:, None, None])
    wide_visible = prefix_visible[:, None, None, :, :]
    sample_count = step_rows.shape[1]
    step_count = step_rows.shape[0]
    step_ids = jnp.arange(step_count, dtype=jnp.int32)
    made_keys = jnp.zeros((sample_count, step_count, kv_local, HEAD), jnp.bfloat16)
    made_values = jnp.zeros((sample_count, step_count, kv_local, HEAD), jnp.bfloat16)
    outputs = []
    for step_index in range(step_count):
        normed_step = norm_rows(step_rows[step_index], norm_gain)
        places_now = length_of + step_index
        step_queries = rotate(
            project(normed_step, full_query, query_bias).reshape(sample_count, heads_local, HEAD),
            places_now,
        ).astype(jnp.bfloat16)
        step_queries = step_queries.reshape(sample_count, kv_local, kv_group, HEAD)
        fresh_keys = rotate(
            project(normed_step, key_weight, key_bias).reshape(sample_count, kv_local, HEAD),
            places_now,
        ).astype(jnp.bfloat16)
        fresh_values = (
            project(normed_step, value_weight, value_bias)
            .astype(jnp.bfloat16)
            .reshape(sample_count, kv_local, HEAD)
        )
        made_keys = made_keys.at[:, step_index].set(fresh_keys)
        made_values = made_values.at[:, step_index].set(fresh_values)
        own_visible = step_ids <= step_index
        far_scores = (
            jnp.einsum(
                "sgqd,pkgd->sgqpk", step_queries, key_grid, preferred_element_type=jnp.float32
            )
            * factor
        )
        far_scores = jnp.where(wide_visible, far_scores, MASKED)
        near_scores = (
            jnp.einsum(
                "sgqd,stgd->sgqt", step_queries, made_keys, preferred_element_type=jnp.float32
            )
            * factor
        )
        near_scores = jnp.where(own_visible, near_scores, MASKED)
        highest_now = jnp.maximum(jnp.max(far_scores, axis=(3, 4)), jnp.max(near_scores, axis=-1))
        far_weights = jnp.where(
            wide_visible, jnp.exp(far_scores - highest_now[..., None, None]), 0.0
        )
        near_weights = jnp.where(own_visible, jnp.exp(near_scores - highest_now[..., None]), 0.0)
        totals_now = jnp.sum(far_weights, axis=(3, 4)) + jnp.sum(near_weights, axis=-1)
        blended_now = jnp.einsum(
            "sgqpk,pkgd->sgqd",
            far_weights.astype(jnp.bfloat16),
            value_grid,
            preferred_element_type=jnp.float32,
        )
        blended_now = blended_now + jnp.einsum(
            "sgqt,stgd->sgqd",
            near_weights.astype(jnp.bfloat16),
            made_values,
            preferred_element_type=jnp.float32,
        )
        step_attention = (
            (blended_now / totals_now[..., None])
            .astype(jnp.bfloat16)
            .reshape(sample_count, heads_local * HEAD)
        )
        outputs.append(step_attention)
    stacked = jnp.stack(outputs)
    decode_terms = jnp.dot(stacked, full_out, preferred_element_type=jnp.float32)
    dec_out = sum_at_owner(decode_terms.astype(jnp.bfloat16), "tp", 2).astype(jnp.bfloat16)
    return (span_out, dec_out)


def solution(mesh):
    return jax.shard_map(
        local,
        mesh=mesh,
        in_specs=(
            P(None, "ctx", None),
            P(None, "ctx", None),
            P(),
            P("ctx"),
            P(),
            P("ctx", "tp"),
            P(None, "tp"),
            P(None, "tp"),
            P("tp"),
            P("tp"),
            P("tp"),
            P("tp", "ctx"),
            P(None, "ctx", "tp"),
            P(None, "ctx", "tp"),
        ),
        out_specs=(P(None, "ctx", "tp"), P(None, "ctx", "tp")),
        check_vma=False,
    )
```

profile of v0, /device:TPU:33, one launch (start us, length us, event | category | flops | bytes accessed | tf_op | source)
XLA Modules:
  0.0 850.7 jit_solution(219215414746392253)
XLA Ops:
  7.3 1.8 pad_maximum_fusion
  9.2 1.2 fusion.129
  10.4 1.7 fusion.62
  12.2 1.4 fusion.63
  13.6 0.7 maximum_maximum_fusion
  14.9 0.3 fusion.118
  15.3 0.3 fusion.107
  15.8 0.3 fusion.104
  16.1 0.3 fusion.105
  16.4 0.3 fusion.106
  17.5 2.0 broadcast_compare_fusion
  19.4 341.8 %all-gather.3.cloned.1.call-done = bf16[3584,1792]{1,0:T(8,128)(2,1)} async-done(((bf16[56,1792]{1,0:T(8,128)(2,1)}), bf16[3584,1792]{1,0:T(8,128)(2,1)}) %all-gather.3.cloned.1.call-update) | async-done | bytes 12845072 | tf_op jit(solution)/shard_map/all_gather | solution.py:22
  361.2 3.8 fusion.91
  365.1 3.8 fusion.88
  368.9 3.8 fusion.94
  372.7 3.8 fusion.97
  376.9 350.5 %all-gather.5.cloned.1.call-done = bf16[4,6144,128]{2,1,0:T(8,128)(2,1)} async-done(((bf16[4,96,128]{2,1,0:T(8,128)(2,1)}), bf16[4,6144,128]{2,1,0:T(8,128)(2,1)}) %all-gather.5.cloned.1.call-update) | async-done | bytes 6291472 | tf_op jit(solution)/shard_map/all_gather | solution.py:35
  727.4 3.3 fusion.310
  731.1 1.3 fusion.312
  732.8 1.3 fusion.314
  734.2 0.8 fusion.309
  735.0 1.3 fusion.308
  736.5 1.8 fusion.51
  738.3 0.6 fusion.64
  738.9 0.2 fusion.87
  739.2 0.3 fusion.117
  739.6 0.8 fusion.67
  740.4 0.2 fusion.86
  740.6 0.3 fusion.115
  741.0 0.6 fusion.70
  741.6 0.2 fusion.85
  741.8 0.3 fusion.113
  742.2 4.1 fusion.59
  746.9 4.8 fusion.307
  751.7 3.0 fusion
  754.8 5.2 fusion.124
  760.2 3.0 fusion.73
  763.2 0.2 fusion.84
  763.5 4.7 fusion.19
  768.2 0.7 copy.96
  768.9 47.9 %all-to-all-start.1 = ((bf16[4,4,4,896]{3,2,1,0:T(4,128)(2,1)}), bf16[4,4,4,896]{3,2,1,0:T(4,128)(2,1)S(1)}, u32[]{:S(2)}, u32[]{:S(2)}) async-start(bf16[4,4,4,896]{3,2,1,0:T(4,128)(2,1)} %bitcast.277), calls=%async_computation.1 | async-start | bytes 229376 | tf_op jit(solution)/shard_map/all_to_all | solution.py:46
  816.7 4.9 fusion.18
  821.6 0.8 copy.95
  822.5 1.6 all-to-all-done.1
  824.1 5.6 all-to-all-start
  829.7 0.7 reduce_sum.175
  830.3 12.8 %all-to-all-done = bf16[4,2,32,896]{3,2,1,0:T(8,128)(2,1)S(1)} async-done(((bf16[4,2,32,896]{3,2,1,0:T(8,128)(2,1)}), bf16[4,2,32,896]{3,2,1,0:T(8,128)(2,1)S(1)}, u32[]{:S(2)}, u32[]{:S(2)}) %all-to-all-start) | async-done | bytes 458784 | tf_op jit(solution)/shard_map/all_to_all | solution.py:46
  843.2 0.7 reduce_sum.161
  (104 shorter events, 4.3 us)
Async XLA Ops:
  7.2 5.1 copy-start
  7.2 7.7 copy-start.3
  7.2 8.1 copy-start.1
  7.2 8.1 copy-start.10
  7.2 7.6 copy-start.11
  7.2 6.4 copy-start.8
  7.2 6.4 copy-start.9
  7.3 7.4 copy-start.4
  7.3 7.9 copy-start.13
  7.3 7.9 copy-start.17
  7.3 354.0 %all-gather.3.cloned.1.call-start = ((), (), s32[]{:S(2)}) async-start(), calls=%async_computation.2 | async-start | bytes 13045760 | tf_op jit(solution)/shard_map/all_gather | solution.py:22
  9.1 718.3 %all-gather.5.cloned.1.call-start = ((), (), s32[]{:S(2)}) async-start(), calls=%async_computation.3 | async-start | bytes 6389760 | tf_op jit(solution)/shard_map/all_gather | solution.py:35
  14.6 719.6 %copy-start.14 = (pred[4]{0:T(512)(128)(4,1)}, pred[4]{0:T(512)(128)(4,1)S(1)}, u32[]{:S(2)}) copy-start(pred[4]{0:T(512)(128)(4,1)S(1)} %iota_compare_fusion.2) | copy-start | bytes 16
  14.9 346.4 %copy-start.7 = (f32[896]{0:T(1024)S(1)}, f32[896]{0:T(1024)}, u32[]{:S(2)}) copy-start(f32[896]{0:T(1024)} %param.38) | copy-start | bytes 10756
  727.4 3.7 copy-start.16
  736.3 2.0 copy-start.5
  740.9 1.3 copy-start.6
  746.9 4.9 copy-start.2
  754.7 5.4 copy-start.12
  754.7 5.4 copy-start.15
  768.9 55.2 %all-to-all-start.1 = ((bf16[4,4,4,896]{3,2,1,0:T(4,128)(2,1)}), bf16[4,4,4,896]{3,2,1,0:T(4,128)(2,1)S(1)}, u32[]{:S(2)}, u32[]{:S(2)}) async-start(bf16[4,4,4,896]{3,2,1,0:T(4,128)(2,1)} %bitcast.277), calls=%async_computation.1 | async-start | bytes 229376 | tf_op jit(solution)/shard_map/all_to_all | solution.py:46
  824.1 19.1 %all-to-all-start = ((bf16[4,2,32,896]{3,2,1,0:T(8,128)(2,1)}), bf16[4,2,32,896]{3,2,1,0:T(8,128)(2,1)S(1)}, u32[]{:S(2)}, u32[]{:S(2)}) async-start(bf16[4,2,32,896]{3,2,1,0:T(8,128)(2,1)} %bitcast.275), calls=%async_computation | async-start | bytes 917504 | tf_op jit(solution)/shard_map/all_to_all | solution.py:46
Sparse Core Ops, SparseCore 0:
  9.9 351.3 all-gather.2
  363.6 363.7 all-gather.4
where the time goes:
time: 853 us; the launch traced here: 851 us
  waiting for transfers between devices  707 us (83%)
  matrix products  58.9 us (7%)
  starting transfers between devices  53.5 us (6%)
  between operations  14.6 us (2%)
  other arithmetic  14.3 us (2%)
    all_gather x1, waiting for transfers between devices, sent_together(): filled = lax.all_gather(both, axis, axis=dim, tiled=True)  351 us
    all_gather x1, waiting for transfers between devices, turned_gather(): filled = lax.all_gather(both, axis, axis=0, tiled=True)  342 us
    all_to_all x2, starting transfers between devices, sum_at_owner(): lax.all_to_all(parts, axis, split_axis=0, concat_axis=0, tiled=True)  53.5 us
    dot_general x15, matrix products, project(): return jnp.dot(normed, weight, preferred_element_type=jnp.float32) + bias  24.7 us
  transfers between devices with their start and end apart: 4, of which 4 were waited for; matrix products, arithmetic and copies ran while one was open for 4% of the time, Pallas kernels for 0%

commit v1 on v0

--- a/solution.py
+++ b/solution.py
@@ -1,8 +1,11 @@
+import functools
 import math
 
 import jax
 import jax.numpy as jnp
 from jax import lax
+from jax.experimental import pallas as pl
+from jax.experimental.pallas import tpu as pltpu
 from jax.sharding import PartitionSpec as P
 
 HEADS = 28
@@ -15,25 +18,139 @@
 MASKED = -1e30
 
 
-def turned_gather(arrays, axis, dims):
-    turned = [jnp.moveaxis(a, dim, 0) for a, dim in zip(arrays, dims)]
-    widths = [t[0].size for t in turned]
-    both = jnp.concatenate([t.reshape(-1, w) for t, w in zip(turned, widths)], axis=1)
-    filled = lax.all_gather(both, axis, axis=0, tiled=True)
-    parts = jnp.split(filled, [sum(widths[:k]) for k in range(1, len(widths))], axis=1)
-    return tuple(
-        (
-            jnp.moveaxis(b.reshape(-1, *t.shape[1:]), 0, dim)
-            for b, t, dim in zip(parts, turned, dims)
-        )
-    )
-
-
-def sent_together(arrays, axis, dim, along):
-    widths = [a.shape[along] for a in arrays]
-    both = jnp.concatenate(arrays, axis=along)
-    filled = lax.all_gather(both, axis, axis=dim, tiled=True)
-    return tuple(jnp.split(filled, [sum(widths[:k]) for k in range(1, len(widths))], axis=along))
+MESH_ID = pl.DeviceIdType.MESH
+RING = 4
+SLOTS = 13
+
+
+def gather_kernel(leads, orders, pairs, *refs):
+    count = len(leads)
+    blocks, fulls = refs[:count], refs[count : 2 * count]
+    local_sem, send_sem, recv_sem = refs[2 * count :]
+    me = lax.axis_index("ctx")
+    place = {"x": me // 16, "y": lax.rem(me // 4, RING), "z": lax.rem(me, RING)}
+
+    def moved(axis, by):
+        there = dict(place)
+        there[axis] = lax.rem(place[axis] + by + RING, RING)
+        return there
+
+    def device(there):
+        return {"ctx": (there["x"] * RING + there["y"]) * RING + there["z"]}
+
+    def part(c, **where):
+        index = tuple(where.get(axis, slice(None)) for axis in "xyz")
+        return fulls[c].at[(slice(None),) * leads[c] + index]
+
+    def copy(c, slot, source, target, there):
+        return pltpu.make_async_remote_copy(
+            src_ref=source,
+            dst_ref=target,
+            send_sem=send_sem.at[c, slot],
+            recv_sem=recv_sem.at[c, slot],
+            device_id=device(there),
+            device_id_type=MESH_ID,
+        )
+
+    copies = {}
+
+    def begin(c, slot, source, target, there):
+        copies[c, slot] = copy(c, slot, source, target, there)
+        copies[c, slot].start()
+
+    def arrived(c, *slots):
+        for slot in slots:
+            copies[c, slot].wait_recv()
+
+    peers = [moved("z", by) for by in (1, 2, 3)]
+    peers += [moved(axis, by) for axis in "xy" for by in (1, -1)]
+    barrier = pltpu.get_barrier_semaphore()
+    for peer in peers:
+        pl.semaphore_signal(barrier, inc=1, device_id=device(peer), device_id_type=MESH_ID)
+    pl.semaphore_wait(barrier, len(peers))
+
+    own = []
+    for c in range(count):
+        mine = part(c, **place)
+        for by in (1, 2, 3):
+            begin(c, by - 1, blocks[c], mine, moved("z", by))
+        kept = pltpu.make_async_copy(blocks[c], mine, local_sem.at[c])
+        kept.start()
+        own.append(kept)
+
+    low, high = pl.ds(0, 2), pl.ds(2, 2)
+
+    def middle(c):
+        axis = orders[c][0]
+        own[c].wait()
+        arrived(c, 0, 1, 2)
+        slab = part(c, x=place["x"], y=place["y"])
+        begin(c, 3, slab, slab, moved(axis, 1))
+        begin(c, 4, slab, slab, moved(axis, -1))
+
+    def middle_on(c):
+        axis = orders[c][0]
+        other = "y" if axis == "x" else "x"
+        before, after = moved(axis, -1), moved(axis, 1)
+        arrived(c, 3)
+        slab = part(c, **{axis: before[axis], other: place[other], "z": low})
+        begin(c, 5, slab, slab, after)
+        arrived(c, 4)
+        slab = part(c, **{axis: after[axis], other: place[other], "z": high})
+        begin(c, 6, slab, slab, before)
+
+    def last(c):
+        inner, axis = orders[c]
+        before, after = moved(axis, -1), moved(axis, 1)
+        arrived(c, 5, 6)
+        first = part(c, **{axis: place[axis], inner: low})
+        second = part(c, **{axis: place[axis], inner: high})
+        begin(c, 7, first, first, after)
+        begin(c, 8, second, second, before)
+        begin(c, 9, second, second, after)
+        begin(c, 10, first, first, before)
+
+    def last_on(c):
+        inner, axis = orders[c]
+        before, after = moved(axis, -1), moved(axis, 1)
+        arrived(c, 7)
+        slab = part(c, **{axis: before[axis], inner: low})
+        begin(c, 11, slab, slab, after)
+        arrived(c, 8)
+        slab = part(c, **{axis: after[axis], inner: high})
+        begin(c, 12, slab, slab, before)
+
+    stages = (middle, middle_on, last, last_on)
+    for tick in range(2 * len(pairs) + 2):
+        for number in range(len(pairs)):
+            stage = tick - 2 * number
+            if 0 <= stage < 4:
+                for c in pairs[number]:
+                    stages[stage](c)
+    for c in range(count):
+        arrived(c, 9, 10, 11, 12)
+        for slot in range(SLOTS):
+            copies[c, slot].wait_send()
+
+
+def gather(blocks, leads, orders, pairs):
+    count = len(blocks)
+    shapes = [
+        jax.ShapeDtypeStruct(b.shape[:k] + (RING,) * 3 + b.shape[k:], b.dtype)
+        for b, k in zip(blocks, leads)
+    ]
+    return pl.pallas_call(
+        functools.partial(gather_kernel, leads, orders, pairs),
+        out_shape=shapes,
+        in_specs=[pl.BlockSpec(memory_space=pltpu.VMEM)] * count,
+        out_specs=[pl.BlockSpec(memory_space=pl.ANY)] * count,
+        scratch_shapes=[
+            pltpu.SemaphoreType.DMA((count,)),
+            pltpu.SemaphoreType.DMA((count, SLOTS)),
+            pltpu.SemaphoreType.DMA((count, SLOTS)),
+        ],
+        compiler_params=pltpu.CompilerParams(collective_id=0, has_side_effects=True),
+    )(*blocks)
 
 
 def in_blocks(x, dim, length):
@@ -109,14 +226,11 @@
     heads_local = kv_local * kv_group
     prefix_all = prefix_dev * cycle_size
     factor = HEAD ** (-0.5)
-    full_query, full_out = turned_gather((query_weight, out_weight), "ctx", (0, 1))
+    cut = 4 * HEAD
+    out_turned = out_weight.T
     normed = norm_rows(span_rows, norm_gain)
     span_places = prefix_all + cycle_place * span_dev + jnp.arange(span_dev, dtype=jnp.int32)
     grid_places = jnp.broadcast_to(span_places, (prompt_count, span_dev))
-    queries = rotate(
-        project(normed, full_query, query_bias).reshape(prompt_count, span_dev, heads_local, HEAD),
-        grid_places,
-    ).astype(jnp.bfloat16)
     new_keys = rotate(
         project(normed, key_weight, key_bias).reshape(prompt_count, span_dev, kv_local, HEAD),
         grid_places,
@@ -126,6 +240,46 @@
         [cache_keys, new_keys.reshape(prompt_count, span_dev, kv_local * HEAD)], axis=1
     )
     value_block = jnp.concatenate([cache_values, new_values], axis=1)
+    blocks = [
+        query_weight[:, :cut],
+        query_weight[:, cut:],
+        key_block,
+        value_block,
+        out_turned[:, :cut],
+        out_turned[:, cut:],
+    ]
+    first, second = ("y", "x"), ("x", "y")
+    query_low, query_high, key_all, value_all, out_low, out_high = gather(
+        blocks,
+        (0, 0, 1, 1, 0, 0),
+        (first, second, first, second, second, first),
+        ((0, 1), (2, 3), (4, 5)),
+    )
+    width = query_weight.shape[0] * cycle_size
+    key_all = key_all.reshape(prompt_count, -1, HEAD)
+    value_all = value_all.reshape(prompt_count, -1, HEAD)
+    query_low, query_high = query_low.reshape(width, -1), query_high.reshape(width, -1)
+    out_low, out_high = out_low.reshape(width, -1), out_high.reshape(width, -1)
+
+    def project_query(rows):
+        sums = [
+            jnp.dot(rows, half, preferred_element_type=jnp.float32)
+            for half in (query_low, query_high)
+        ]
+        return jnp.concatenate(sums, axis=-1) + query_bias
+
+    def project_out(rows):
+        halves = ((rows[..., :cut], out_low), (rows[..., cut:], out_high))
+        sums = [
+            jnp.einsum("...k,nk->...n", part, half, preferred_element_type=jnp.float32)
+            for part, half in halves
+        ]
+        return sums[0] + sums[1]
+
+    queries = rotate(
+        project_query(normed).reshape(prompt_count, span_dev, heads_local, HEAD),
+        grid_places,
+    ).astype(jnp.bfloat16)
     query_rows = (
         queries.reshape(prompt_count, span_dev, kv_local, kv_group, HEAD)
         .transpose(0, 2, 1, 3, 4)
@@ -133,7 +287,6 @@
     )
     query_places = jnp.repeat(span_places, kv_group)
     row_count = span_dev * kv_group
-    key_all, value_all = sent_together((key_block, value_block), "ctx", 1, 0)
     highest = jnp.full((prompt_count, kv_local, row_count), MASKED, jnp.float32)
     count = key_all.shape[1]
     places = key_positions(count, prefix_dev, span_dev, prefix_all)
@@ -163,7 +316,7 @@
         .transpose(0, 2, 1, 3, 4)
         .reshape(prompt_count, span_dev, heads_local * HEAD)
     )
-    span_terms = jnp.dot(span_attention, full_out, preferred_element_type=jnp.float32)
+    span_terms = project_out(span_attention)
     span_out = sum_at_owner(span_terms.astype(jnp.bfloat16), "tp", 2).astype(jnp.bfloat16)
     gathered_rows = key_all.shape[1]
     key_grid = key_all.reshape(prompt_count, gathered_rows, kv_local, HEAD)
@@ -183,7 +336,7 @@
         normed_step = norm_rows(step_rows[step_index], norm_gain)
         places_now = length_of + step_index
         step_queries = rotate(
-            project(normed_step, full_query, query_bias).reshape(sample_count, heads_local, HEAD),
+            project_query(normed_step).reshape(sample_count, heads_local, HEAD),
             places_now,
         ).astype(jnp.bfloat16)
         step_queries = step_queries.reshape(sample_count, kv_local, kv_group, HEAD)
@@ -238,7 +391,7 @@
         )
         outputs.append(step_attention)
     stacked = jnp.stack(outputs)
-    decode_terms = jnp.dot(stacked, full_out, preferred_element_type=jnp.float32)
+    decode_terms = project_out(stacked)
     dec_out = sum_at_owner(decode_terms.astype(jnp.bfloat16), "tp", 2).astype(jnp.bfloat16)
     return (span_out, dec_out)
 

time: 853 us -> 228 us (0.27)
  waiting for transfers between devices: 707 us -> 13.1 us
  Pallas kernels: 0 us -> 121 us
  starting transfers between devices: 53.5 us -> 20.1 us
  between operations: 14.6 us -> 1.24 us
    all_gather x2 -> x0, waiting for transfers between devices: 692 us -> none  [the longest x1 351 us: sent_together(): filled = lax.all_gather(both, axis, axis=dim, tiled=True)]
    pallas_call x0 -> x1, Pallas kernels: none -> 121 us  [gather(): pl.pallas_call(functools.partial(gather_kernel, leads, orders, pairs), ou...]
    all_to_all x2, starting transfers between devices: 53.5 us -> 20.1 us  [sum_at_owner(): lax.all_to_all(parts, axis, split_axis=0, concat_axis=0, tiled=True)]
    dot_general x15 -> x10, matrix products: 24.7 us -> 4.75 us  [project(): return jnp.dot(normed, weight, preferred_element_type=jnp.float32) + bias]
    dot_general x2 -> x14, matrix products: 9.56 us -> 18.3 us  [the longest x10 9.8 us: project_query(): jnp.dot(rows, half, preferred_element_type=jnp.float32)]
  transfers between devices with their start and end apart: 4 -> 2, of which waited for: 4 -> 1; matrix products, arithmetic and copies ran while one was open for 4% -> 11% of each run, Pallas kernels for 0% -> 0%
where the time goes in v1:
time: 228 us
  Pallas kernels  121 us (53%)
  matrix products  50.7 us (22%)
  starting transfers between devices  20.1 us (9%)
  other arithmetic  14.5 us (6%)
  waiting for transfers between devices  13.1 us (6%)
  local copies, waits for them, and re-layouts  6.87 us (3%)
    pallas_call x1, Pallas kernels, gather(): pl.pallas_call(functools.partial(gather_kernel, leads, orders, pairs), ou...  121 us
    all_to_all x2, starting transfers between devices, sum_at_owner(): lax.all_to_all(parts, axis, split_axis=0, concat_axis=0, tiled=True)  20.1 us
    all_to_all x2, waiting for transfers between devices, sum_at_owner(): lax.all_to_all(parts, axis, split_axis=0, concat_axis=0, tiled=True)  13.1 us
    dot_general x10, matrix products, project_query(): jnp.dot(rows, half, preferred_element_type=jnp.float32)  9.8 us
    dot_general x4, matrix products, local(): jnp.einsum('sgqpk,pkgd->sgqd', far_weights.astype(jnp.bfloat16), value_gr...  9.23 us
    dot_general x4, matrix products, project_out(): jnp.einsum('...k,nk->...n', part, half, preferred_element_type=jnp.float32)  8.52 us
    dot_general x4, matrix products, local(): jnp.einsum('sgqd,pkgd->sgqpk', step_queries, key_grid, preferred_element_...  7.22 us
    dot_general x1, matrix products, local(): jnp.einsum('pgqk,pkgd->pgqd', weights.astype(jnp.bfloat16), value_grid, p...  4.81 us
  transfers between devices with their start and end apart: 2, of which 1 were waited for; matrix products, arithmetic and copies ran while one was open for 11% of the time, Pallas kernels for 0%

profile of v1, /device:TPU:33, one launch (start us, length us, event | category | flops | bytes accessed | tf_op | source)
XLA Modules:
  0.0 227.5 jit_solution(13343672807626630222)
XLA Ops:
  0.8 1.3 fusion.63
  2.2 1.0 fusion.122
  3.2 1.0 fusion.56
  4.2 1.4 fusion.25
  6.0 0.3 fusion.24
  6.3 0.6 slice.329.refs_5_
  6.9 0.6 slice.328.refs_4_
  7.6 0.6 slice.295.refs_1_
  8.2 0.6 slice.294.refs_0_
  9.4 0.6 pad_maximum_fusion.1.refs_3_
  10.2 0.7 maximum_maximum_fusion.refs_2_
  10.9 121.1 %shard_map.149 = (bf16[4,4,4,56,512]{4,3,2,1,0:T(8,128)(2,1)}, bf16[4,4,4,56,384]{4,3,2,1,0:T(8,128)(2,1)}, bf16[2,4,4,4,96,128]{5,4,3,2,1,0:T(8,128)(2,1)}, bf1...) custom-call(bf16[56,512]{1,0:T(8,128)(2,1)} %slice.294.refs_0_, ...), custom_call_target="tpu_custom_call" | custom-call | tf_op jit(solution)/shard_map/pallas_call | solution.py:142
  132.0 2.4 %fusion.258 = f32[4,384]{1,0:T(4,128)S(1)} fusion(bf16[3584,384]{1,0:T(8,128)(2,1)} %bitcast.322, f32[4]{0:T(128)S(1)} %get-tuple-element.187, f32[3584]{0:T(1024)S(1)} %copy-done.8, bf16[4,4,3584]{2,1,0:T(4,128)(2,1)S(1)} %copy-done.10), kind=kOutput, calls=%fused_computation.367 | convolution fusion | flops 11067392 | bytes 2804224 | tf_op jit(solution)/shard_map/dot_general | solution.py:266
  134.6 0.5 fusion.254
  135.1 0.5 fusion.250
  136.0 0.5 fusion.262
  136.5 0.7 copy-done.1
  137.2 0.6 fusion.252
  137.8 0.6 fusion.260
  138.4 0.6 fusion.256
  139.1 0.6 fusion.264
  140.9 3.3 %fusion.275 = (f32[4,7]{1,0:T(4,128)S(1)}, f32[4,1,7,2,6144]{4,2,0,3,1:T(8,128)S(1)}) fusion(bf16[2,6144,128,1]{2,1,3,0:T(8,128)(2,1)} %bitcast.344, bf16[4,7,64]{2,1,0:T(8,128)(2,1)S(1)} %get-tuple-element.129, bf16[4,7,64]{2,1,0:T(8,128)(2,1)S(1)} %get-tuple-element.128, pred[4,2,6144]{2,0,1:T(4,128)(4,1)S(1)} %broadcast_and_fusion), kind=kOutput, calls=%fused_computation.372 | convolution fusion | flops 89126880 | bytes 4578416 | tf_op jit(solution)/shard_map/sgqd,pkgd->sgqpk/dot_general | solution.py:356
  145.2 1.3 fusion.279
  147.5 1.3 fusion.281
  149.8 1.3 fusion.277
  151.6 2.0 fusion.22
  153.6 0.7 fusion.36
  154.3 3.0 %fusion.35 = bf16[4,1,7,128]{3,2,0,1:T(8,128)(2,1)S(1)} fusion(f32[4,1,7,128]{3,2,0,1:T(8,128)S(1)} %convolution_bitcast_fusion.6, bf16[2,6144,128,1]{2,1,3,0:T(8,128)(2,1)} %bitcast.339, f32[4,1,7,2,6144]{4,2,0,3,1:T(8,128)} %copy-done.11, f32[4,7]{1,0:T(4,128)S(1)} %max.53, pred[4,2,6144]{2,0,1:T(4,128)(4,1)S(1)} %broadcast_and_fusion, f32[4,7]{1,0:T(4,128)S(1)} %add.410), kind=kOutput, calls=%fused_computation.59 | convolution fusion | flops 89123328 | bytes 4592864 | tf_op jit(solution)/shard_map/sgqpk,pkgd->sgqd/dot_general | solution.py:375
  157.3 3.0 %fusion.37 = bf16[4,1,7,128]{3,2,0,1:T(8,128)(2,1)S(1)} fusion(f32[4,1,7,128]{3,2,0,1:T(8,128)S(1)} %convolution_bitcast_fusion.4, bf16[2,6144,128,1]{2,1,3,0:T(8,128)(2,1)} %bitcast.340, f32[4,1,7,2,6144]{4,2,0,3,1:T(8,128)} %copy-done.12, f32[4,7]{1,0:T(4,128)S(1)} %max.55, pred[4,2,6144]{2,0,1:T(4,128)(4,1)S(1)} %broadcast_and_fusion, f32[4,7]{1,0:T(4,128)S(1)} %add.428), kind=kOutput, calls=%fused_computation.61 | convolution fusion | flops 89123328 | bytes 4592864 | tf_op jit(solution)/shard_map/sgqpk,pkgd->sgqd/dot_general | solution.py:375
  160.4 2.5 %fusion.34 = bf16[4,1,7,128]{3,2,0,1:T(8,128)(2,1)S(1)} fusion(f32[4,1,7,128]{3,2,0,1:T(8,128)S(1)} %convolution_bitcast_fusion.7, bf16[2,6144,128,1]{2,1,3,0:T(8,128)(2,1)} %bitcast.341, f32[4,1,7,2,6144]{4,2,0,3,1:T(8,128)S(1)} %get-tuple-element.169, f32[4,7]{1,0:T(4,128)S(1)} %max.52, pred[4,2,6144]{2,0,1:T(4,128)(4,1)S(1)} %broadcast_and_fusion, ...), kind=kOutput, calls=%fused_computation.58 | convolution fusion | flops 89123328 | bytes 4592864 | tf_op jit(solution)/shard_map/sgqpk,pkgd->sgqd/dot_general | solution.py:375
  163.0 3.3 %fusion.152 = f32[4,4,3584]{2,1,0:T(4,128)S(1)} fusion(bf16[3584,512,1]{1,0,2:T(8,128)(2,1)} %bitcast.327, bf16[4,4,896]{2,1,0:T(4,128)(2,1)S(1)} %constant_dynamic-update-slice_fusion), kind=kOutput, calls=%fused_computation.203 | convolution fusion | flops 58720256 | bytes 3915776 | tf_op jit(solution)/shard_map/...k,nk->...n/dot_general | solution.py:274
  166.3 0.9 fusion.15
  167.2 0.7 copy.96
  167.9 12.9 %all-to-all-start.1 = ((bf16[4,4,4,896]{3,2,1,0:T(4,128)(2,1)}), bf16[4,4,4,896]{3,2,1,0:T(4,128)(2,1)S(1)}, u32[]{:S(2)}, u32[]{:S(2)}) async-start(bf16[4,4,4,896]{3,2,1,0:T(4,128)(2,1)} %bitcast.316), calls=%async_computation.1 | async-start | bytes 229376 | tf_op jit(solution)/shard_map/all_to_all | solution.py:163
  181.2 2.0 broadcast_compare_fusion
  183.1 2.5 %fusion.91 = f32[2,32,384]{2,1,0:T(8,128)S(1)} fusion(bf16[3584,384,1]{1,0,2:T(8,128)(2,1)} %bitcast.323, bf16[2,32,3584]{2,1,0:T(8,128)(2,1)S(1)} %copy-done.7, f32[3584]{0:T(1024)S(1)} %copy-done.8, f32[2,32]{1,0:T(2,128)S(1)} %add_rsqrt_fusion), kind=kOutput, calls=%fused_computation.125 | convolution fusion | flops 177078272 | bytes 3324160 | tf_op jit(solution)/shard_map/dot_general | solution.py:266
  186.0 0.8 fusion.93
  187.4 0.7 copy-done.9
  188.1 4.5 %fusion.274 = (f32[2,224]{1,0:T(2,128)S(1)}, f32[2,224,6144]{2,1,0:T(8,128)S(1)}) fusion(bf16[2,6144,128]{2,1,0:T(8,128)(2,1)} %bitcast.345, bf16[2,224,64]{2,1,0:T(8,128)(2,1)S(1)} %copy.47, bf16[2,224,64]{2,1,0:T(8,128)(2,1)S(1)} %copy.46, pred[224,6144]{1,0:T(8,128)(4,1)S(1)} %copy-done.9, pred[2,6144]{1,0:T(4,128)(4,1)S(1)} %broadcast_compare_fusion.2), kind=kOutput, calls=%fused_computation.371 | convolution fusion | flops 715882048 | bytes 15660800 | tf_op jit(solution)/shard_map/pgqd,pkgd->pgqk/dot_general | solution.py:296
  192.7 3.0 %fusion = f32[2,224]{1,0:T(2,128)S(1)} fusion(f32[2,224,6144]{2,1,0:T(8,128)S(1)} %get-tuple-element.167, f32[2,224]{1,0:T(2,128)S(1)} %broadcast_maximum_fusion, pred[224,6144]{1,0:T(8,128)(4,1)S(1)} %copy-done.9, pred[2,6144]{1,0:T(4,128)(4,1)S(1)} %broadcast_compare_fusion.2), kind=kLoop, calls=%fused_computation.2 | loop fusion | flops 11009600 | bytes 12402176 | tf_op jit(solution)/shard_map/reduce_sum | solution.py:305
  195.7 4.8 %fusion.60 = bf16[2,224,128]{2,1,0:T(8,128)(2,1)S(1)} fusion(bf16[2,6144,128]{2,1,0:T(8,128)(2,1)} %bitcast.342, f32[2,224,6144]{2,1,0:T(8,128)S(1)} %get-tuple-element.167, f32[2,224]{1,0:T(2,128)S(1)} %broadcast_maximum_fusion, pred[224,6144]{1,0:T(8,128)(4,1)S(1)} %copy-done.9, pred[2,6144]{1,0:T(4,128)(4,1)S(1)} %broadcast_compare_fusion.2, ...), kind=kOutput, calls=%fused_computation.94 | convolution fusion | flops 715767808 | bytes 15662592 | tf_op jit(solution)/shard_map/pgqk,pkgd->pgqd/dot_general | solution.py:306
  200.7 3.4 %fusion.105 = f32[2,32,3584]{2,1,0:T(8,128)S(1)} fusion(bf16[3584,512,1]{1,0,2:T(8,128)(2,1)} %bitcast.328, bf16[2,32,896]{2,1,0:T(8,128)(2,1)S(1)} %reshape_transpose_reshape.4), kind=kOutput, calls=%fused_computation.144 | convolution fusion | flops 234881024 | bytes 4653056 | tf_op jit(solution)/shard_map/...k,nk->...n/dot_general | solution.py:274
  204.1 1.0 fusion.14
  205.1 0.8 copy.95
  205.9 7.2 %all-to-all-start = ((bf16[4,2,32,896]{3,2,1,0:T(8,128)(2,1)}), bf16[4,2,32,896]{3,2,1,0:T(8,128)(2,1)S(1)}, u32[]{:S(2)}, u32[]{:S(2)}) async-start(bf16[4,2,32,896]{3,2,1,0:T(8,128)(2,1)} %bitcast.314), calls=%async_computation | async-start | bytes 917504 | tf_op jit(solution)/shard_map/all_to_all | solution.py:163
  213.1 0.7 reduce_sum.175
  213.8 13.1 %all-to-all-done = bf16[4,2,32,896]{3,2,1,0:T(8,128)(2,1)S(1)} async-done(((bf16[4,2,32,896]{3,2,1,0:T(8,128)(2,1)}), bf16[4,2,32,896]{3,2,1,0:T(8,128)(2,1)S(1)}, u32[]{:S(2)}, u32[]{:S(2)}) %all-to-all-start) | async-done | bytes 458784 | tf_op jit(solution)/shard_map/all_to_all | solution.py:163
  226.8 0.7 reduce_sum.161
  (133 shorter events, 7.7 us)
Async XLA Ops:
  0.6 2.6 %copy-start = (bf16[3584,128]{1,0:T(8,128)(2,1)S(1)}, bf16[3584,128]{1,0:T(8,128)(2,1)}, u32[]{:S(2)}) copy-start(bf16[3584,128]{1,0:T(8,128)(2,1)} %param.37) | copy-start | bytes 2752516
  0.6 5.3 %copy-start.7 = (bf16[2,32,3584]{2,1,0:T(8,128)(2,1)S(1)}, bf16[2,32,3584]{2,1,0:T(8,128)(2,1)}, u32[]{:S(2)}) copy-start(bf16[2,32,3584]{2,1,0:T(8,128)(2,1)} %param.30) | copy-start | bytes 1376260
  0.7 5.0 %copy-start.10 = (bf16[4,4,3584]{2,1,0:T(4,128)(2,1)S(1)}, bf16[4,4,3584]{2,1,0:T(4,128)(2,1)}, u32[]{:S(2)}) copy-start(bf16[4,4,3584]{2,1,0:T(4,128)(2,1)} %param.31) | copy-start | bytes 344068
  0.7 5.0 %copy-start.8 = (f32[3584]{0:T(1024)S(1)}, f32[3584]{0:T(1024)}, u32[]{:S(2)}) copy-start(f32[3584]{0:T(1024)} %param.34) | copy-start | bytes 43012
  0.7 5.0 %copy-start.18 = (f32[128]{0:T(128)S(1)}, f32[128]{0:T(128)}, u32[]{:S(2)}) copy-start(f32[128]{0:T(128)} %param.39) | copy-start | bytes 1540
  0.7 5.0 %copy-start.4 = (bf16[3584,128]{1,0:T(8,128)(2,1)S(1)}, bf16[3584,128]{1,0:T(8,128)(2,1)}, u32[]{:S(2)}) copy-start(bf16[3584,128]{1,0:T(8,128)(2,1)} %param.36) | copy-start | bytes 2752516
  0.7 5.6 %copy-start.13 = (bf16[896,56]{0,1:T(8,128)(2,1)S(1)}, bf16[896,56]{0,1:T(8,128)(2,1)}, u32[]{:S(2)}) copy-start(bf16[896,56]{0,1:T(8,128)(2,1)} %param.41) | copy-start | bytes 301060
  0.8 6.8 %copy-start.14 = (bf16[56,896]{1,0:T(8,128)(2,1)S(1)}, bf16[56,896]{1,0:T(8,128)(2,1)}, u32[]{:S(2)}) copy-start(bf16[56,896]{1,0:T(8,128)(2,1)} %param.35) | copy-start | bytes 301060
  4.2 5.2 %copy-start.15 = (bf16[2,64,128]{2,1,0:T(8,128)(2,1)S(1)}, bf16[2,64,128]{2,1,0:T(8,128)(2,1)}, u32[]{:S(2)}) copy-start(bf16[2,64,128]{2,1,0:T(8,128)(2,1)} %param.43) | copy-start | bytes 98308
  5.7 4.5 %copy-start.16 = (bf16[2,64,128]{2,1,0:T(8,128)(2,1)S(1)}, bf16[2,64,128]{2,1,0:T(8,128)(2,1)}, u32[]{:S(2)}) copy-start(bf16[2,64,128]{2,1,0:T(8,128)(2,1)} %param.42) | copy-start | bytes 98308
  132.0 2.6 %copy-start.3 = (bf16[4,4,4,56,384]{4,3,2,1,0:T(8,128)(2,1)S(1)}, bf16[4,4,4,56,384]{4,3,2,1,0:T(8,128)(2,1)}, u32[]{:S(2)}) copy-start(bf16[4,4,4,56,384]{4,3,2,1,0:T(8,128)(2,1)} %get-tuple-element.105) | copy-start | bytes 8257540
  135.1 2.1 copy-start.1
  139.1 0.7 copy-start.23
  139.1 0.7 copy-start.20
  139.1 1.5 copy-start.17
  140.8 3.7 %copy-start.19 = (f32[128]{0:T(128)S(1)}, f32[128]{0:T(128)}, u32[]{:S(2)}) copy-start(f32[128]{0:T(128)} %param.40) | copy-start | bytes 1540
  140.9 4.3 %copy-start.22 = (bf16[2,4,4,4,96,128]{5,4,3,2,1,0:T(8,128)(2,1)S(1)}, bf16[2,4,4,4,96,128]{5,4,3,2,1,0:T(8,128)(2,1)}, u32[]{:S(2)}) copy-start(bf16[2,4,4,4,96,128]{5,4,3,2,1,0:T(8,128)(2,1)} %get-tuple-element.106) | copy-start | bytes 9437188
  146.4 5.2 %copy-start.11 = (f32[4,1,7,2,6144]{4,2,0,3,1:T(8,128)}, f32[4,1,7,2,6144]{4,2,0,3,1:T(8,128)S(1)}, u32[]{:S(2)}) copy-start(f32[4,1,7,2,6144]{4,2,0,3,1:T(8,128)S(1)} %get-tuple-element.177) | copy-start | bytes 4128772
  151.1 2.5 %copy-start.12 = (f32[4,1,7,2,6144]{4,2,0,3,1:T(8,128)}, f32[4,1,7,2,6144]{4,2,0,3,1:T(8,128)S(1)}, u32[]{:S(2)}) copy-start(f32[4,1,7,2,6144]{4,2,0,3,1:T(8,128)S(1)} %get-tuple-element.173) | copy-start | bytes 4128772
  151.6 2.0 copy-start.21
  162.9 3.4 %copy-start.5 = (bf16[4,4,4,56,384]{4,3,2,1,0:T(8,128)(2,1)S(1)}, bf16[4,4,4,56,384]{4,3,2,1,0:T(8,128)(2,1)}, u32[]{:S(2)}) copy-start(bf16[4,4,4,56,384]{4,3,2,1,0:T(8,128)(2,1)} %get-tuple-element.109) | copy-start | bytes 8257540
  167.9 38.0 %all-to-all-start.1 = ((bf16[4,4,4,896]{3,2,1,0:T(4,128)(2,1)}), bf16[4,4,4,896]{3,2,1,0:T(4,128)(2,1)S(1)}, u32[]{:S(2)}, u32[]{:S(2)}) async-start(bf16[4,4,4,896]{3,2,1,0:T(4,128)(2,1)} %bitcast.316), calls=%async_computation.1 | async-start | bytes 229376 | tf_op jit(solution)/shard_map/all_to_all | solution.py:163
  183.1 2.9 %copy-start.2 = (bf16[4,4,4,56,512]{4,3,2,1,0:T(8,128)(2,1)S(1)}, bf16[4,4,4,56,512]{4,3,2,1,0:T(8,128)(2,1)}, u32[]{:S(2)}) copy-start(bf16[4,4,4,56,512]{4,3,2,1,0:T(8,128)(2,1)} %get-tuple-element.104) | copy-start | bytes 11010052
  186.8 1.3 copy-start.9
  200.7 3.4 %copy-start.6 = (bf16[4,4,4,56,384]{4,3,2,1,0:T(8,128)(2,1)S(1)}, bf16[4,4,4,56,384]{4,3,2,1,0:T(8,128)(2,1)}, u32[]{:S(2)}) copy-start(bf16[4,4,4,56,384]{4,3,2,1,0:T(8,128)(2,1)} %get-tuple-element.109) | copy-start | bytes 8257540
  205.9 20.9 %all-to-all-start = ((bf16[4,2,32,896]{3,2,1,0:T(8,128)(2,1)}), bf16[4,2,32,896]{3,2,1,0:T(8,128)(2,1)S(1)}, u32[]{:S(2)}, u32[]{:S(2)}) async-start(bf16[4,2,32,896]{3,2,1,0:T(8,128)(2,1)} %bitcast.314), calls=%async_computation | async-start | bytes 917504 | tf_op jit(solution)/shard_map/all_to_all | solution.py:163
